TPU v7x, 32 devices: a whole 2x2x4 slice. The times are simulated.
32 devices in a mesh: seq: 8 (over z, core), head: 4 (over y, x).
Axes of the slice: x: 2, y: 2, z: 4, core: 2. Of those that a mesh axis runs over, the one named last changes fastest.
Arguments:
- grad_output: bfloat16 [8192, 4096], P('seq', 'head'), may hold values from -6 to 6
- out_weight: bfloat16 [4096, 8192], P('seq', 'head'), may hold values from -0.0625 to 0.0625
- ssd_out: bfloat16 [8192, 8192], P('seq', 'head'), may hold values from -520 to 520
- gate: bfloat16 [8192, 8192], P('seq', 'head'), may hold values from -5 to 5
- norm_weight: float32 [8192], P('head'), may hold values from 0.5 to 1.5
- time_step: float32 [128, 8192], P('head', 'seq'), may hold values from 0.01 to 0.1
- log_decay: float32 [128, 8192], P('head', 'seq'), may hold values from -0.7 to 0
- state_in: bfloat16 [8192, 8, 128], P('seq'), may hold values from -1.796875 to 1.796875
- state_out: bfloat16 [8192, 8, 128], P('seq'), may hold values from -1.796875 to 1.796875
- skip: float32 [128], P('head'), may hold values from 0.5 to 1.5
Outputs:
- grad_x: bfloat16 [8192, 8192], P('seq', 'head')
- grad_gate: bfloat16 [8192, 8192], P('seq', 'head')
- grad_out_weight: float32 [4096, 8192], P('seq', 'head')
All inputs are finite; a program needn't handle non-finite values.
Results may differ from a plain program's by a relative error of at most 0.014.
Values may be sent and summed in bfloat16 or wider, within the bound.
A program may use at most 192 MiB of HBM per device.

v0:
```python
import math
import jax
import jax.numpy as jnp
from jax import lax
from jax.sharding import PartitionSpec as P

HEADS = 128
GROUPS = 8
BLOCK_LEN = 256
epsilon = 1e-05


def shifted(x, axis, by):
    size = lax.axis_size(axis)
    pairs = [(i, i + by) for i in range(size) if 0 <= i + by < size]
    return lax.ppermute(x, axis, pairs)


def on_device(
    grad_output,
    out_weight,
    ssd_out,
    gate,
    norm_weight,
    time_step,
    log_decay,
    state_in,
    state_out,
    skip,
):
    tok_rows = ssd_out.shape[0]
    local_width = ssd_out.shape[1]
    total_width = local_width * lax.axis_size("head")
    full_grad = lax.all_gather(grad_output, "head", axis=1, tiled=True)
    values = ssd_out.astype(jnp.float32)
    gate_values = gate.astype(jnp.float32)
    sigmoid_gate = jax.nn.sigmoid(gate_values)
    silu_gate = gate_values * sigmoid_gate
    gated_values = values * silu_gate
    local_squares = jnp.sum(gated_values * gated_values, axis=1)
    squares = lax.psum(local_squares, "head")
    columns = full_grad
    normed_grad = jnp.dot(
        columns,
        lax.all_gather(out_weight, "seq", axis=0, tiled=True),
        preferred_element_type=jnp.float32,
    )
    weighted = lax.psum(jnp.sum(norm_weight * normed_grad * gated_values, axis=1), "head")
    inverse_rms = lax.rsqrt(squares[:, None] / total_width + epsilon)
    normed = (gated_values * inverse_rms * norm_weight).astype(jnp.bfloat16)
    gated_grad = (
        inverse_rms * norm_weight * normed_grad
        - gated_values * inverse_rms**3 * weighted[:, None] / total_width
    )
    grad_gate = (
        gated_grad * values * sigmoid_gate * (1.0 + gate_values * (1.0 - sigmoid_gate))
    ).astype(jnp.bfloat16)
    grad_ssd = (gated_grad * silu_gate).astype(jnp.bfloat16)
    columns = full_grad
    weight_sum = lax.psum_scatter(
        lax.dot_general(
            columns, normed, (((0,), (0,)), ((), ())), preferred_element_type=jnp.float32
        ),
        "seq",
        scatter_dimension=0,
        tiled=True,
    )
    grad_out_weight = weight_sum * (1.0 / math.sqrt(tok_rows * lax.axis_size("seq")))
    heads_here = time_step.shape[0]
    head_width = local_width // heads_here
    blocks = tok_rows // BLOCK_LEN
    state_width = state_in.shape[2]
    group_count = state_in.shape[1]
    first_head = lax.axis_index("head") * heads_here
    head_ids = first_head + jnp.arange(heads_here, dtype=jnp.int32)
    group_ids = head_ids // (HEADS // GROUPS)
    group_pick = (group_ids[:, None] == jnp.arange(group_count, dtype=jnp.int32)[None, :]).astype(
        jnp.bfloat16
    )
    b_heads = jnp.einsum(
        "tgn,hg->htn", state_in, group_pick, preferred_element_type=jnp.float32
    ).astype(jnp.bfloat16)
    b_heads = b_heads.reshape(heads_here, blocks, BLOCK_LEN, state_width)
    c_heads = jnp.einsum(
        "tgn,hg->htn", state_out, group_pick, preferred_element_type=jnp.float32
    ).astype(jnp.bfloat16)
    c_heads = c_heads.reshape(heads_here, blocks, BLOCK_LEN, state_width)
    grad_heads = grad_ssd.reshape(tok_rows, heads_here, head_width).transpose(1, 0, 2)
    grad_heads = grad_heads.reshape(heads_here, blocks, BLOCK_LEN, head_width)
    cumulative = jnp.cumsum(log_decay.reshape(heads_here, blocks, BLOCK_LEN), axis=2)
    block_total = cumulative[..., -1]
    sequence_indices = jnp.arange(BLOCK_LEN)
    upper_mask = sequence_indices[None, :] >= sequence_indices[:, None]
    scores = jnp.einsum("hktn,hksn->hkts", b_heads, c_heads, preferred_element_type=jnp.float32)
    log_gap = cumulative[..., None, :] - cumulative[..., :, None]
    block_weights = jnp.where(upper_mask, scores * jnp.exp(jnp.minimum(log_gap, 0.0)), 0.0).astype(
        jnp.bfloat16
    )
    within = jnp.einsum(
        "hkts,hksp->hktp", block_weights, grad_heads, preferred_element_type=jnp.float32
    )
    grad_float = grad_heads.astype(jnp.float32)
    scaled = (jnp.exp(cumulative)[..., None] * grad_float).astype(jnp.bfloat16)
    block_state = jnp.einsum("hksp,hksn->hkpn", scaled, c_heads, preferred_element_type=jnp.float32)

    def fold_block(carried, inputs):
        state_now, total_now = inputs
        return (state_now + jnp.exp(total_now)[:, None, None] * carried, carried)

    zero_state = jnp.zeros((heads_here, head_width, state_width), jnp.float32)
    summary, inside = lax.scan(
        fold_block, zero_state, (block_state.transpose(1, 0, 2, 3), block_total.T), reverse=True
    )
    decay_total = jnp.exp(jnp.sum(block_total, axis=1))
    tail_decay = jnp.exp(
        jnp.sum(block_total, axis=1, keepdims=True) - jnp.cumsum(block_total, axis=1)
    )

    def pass_back(relay_turn, carried_state):
        return shifted(
            (summary + decay_total[:, None, None] * carried_state).astype(jnp.bfloat16), "seq", -1
        ).astype(jnp.float32)

    remote = lax.fori_loop(0, lax.axis_size("seq") - 1, pass_back, zero_state)
    full_states = inside.transpose(1, 0, 2, 3) + tail_decay[..., None, None] * remote[:, None]
    carry_low = full_states.astype(jnp.bfloat16)
    across = jnp.einsum("hkpn,hktn->hktp", carry_low, b_heads, preferred_element_type=jnp.float32)
    across = across * jnp.exp(block_total[..., None] - cumulative)[..., None]
    step_sizes = time_step.reshape(heads_here, blocks, BLOCK_LEN)
    grad_head = step_sizes[..., None] * (within + across) + skip[:, None, None, None] * grad_float
    grad_x = (
        grad_head.reshape(heads_here, tok_rows, head_width)
        .transpose(1, 0, 2)
        .reshape(tok_rows, local_width)
    )
    return (grad_x.astype(jnp.bfloat16), grad_gate, grad_out_weight)


def solution(mesh):
    return jax.shard_map(
        on_device,
        mesh=mesh,
        in_specs=(
            P("seq", "head"),
            P("seq", "head"),
            P("seq", "head"),
            P("seq", "head"),
            P("head"),
            P("head", "seq"),
            P("head", "seq"),
            P("seq", None, None),
            P("seq", None, None),
            P("head"),
        ),
        out_specs=(P("seq", "head"), P("seq", "head"), P("seq", "head")),
        check_vma=False,
    )
```

profile of v0, /device:TPU:0, one launch (start us, length us, event | category | flops | bytes accessed | tf_op | source)
XLA Modules:
  0.0 695.3 jit_solution(3840516232914218780)
XLA Ops:
  8.0 0.7 all-gather.5.cloned.1.call-update
  8.7 91.3 %all-gather.3.cloned.1.call-done = bf16[1024,4096]{1,0:T(8,128)(2,1)} async-done(((bf16[1024,1024]{1,0:T(8,128)(2,1)}), bf16[1024,4096]{1,0:T(8,128)(2,1)}) %all-gather.3.cloned.1.call-update) | async-done | bytes 8388624 | tf_op jit(solution)/shard_map/all_gather | solution.py:34
  100.1 152.7 %all-gather.5.cloned.1.call-done = bf16[4096,2048]{1,0:T(8,128)(2,1)} async-done(((bf16[512,2048]{1,0:T(8,128)(2,1)}), bf16[4096,2048]{1,0:T(8,128)(2,1)}) %all-gather.5.cloned.1.call-update) | async-done | bytes 16777232 | tf_op jit(solution)/shard_map/all_gather | solution.py:45
  252.8 27.2 %multiply_reduce_fusion.1 = (f32[1024]{0:T(1024)S(1)}, f32[1024]{0:T(1024)S(1)}, f32[1024,2048]{1,0:T(8,128)}) fusion(bf16[1024,2048]{1,0:T(8,128)(2,1)} %param.16, bf16[1024,2048]{1,0:T(8,128)(2,1)} %param.17, f32[2048]{0:T(1024)} %param.18, bf16[1024,4096]{1,0:T(8,128)(2,1)} %all-gather.3.cloned.1.call-done, ...), kind=kOutput, calls=%fused_computation.34 | convolution fusion | flops 17205035008 | bytes 41959424 | tf_op jit(solution)/shard_map/dot_general | solution.py:43
  279.9 10.5 %all-reduce = (f32[1024]{0:T(1024)}, f32[1024]{0:T(1024)S(1)}) all-reduce(f32[1024]{0:T(1024)S(1)} %get-tuple-element.190, f32[1024]{0:T(1024)S(1)} %get-tuple-element.189), channel_id=1, replica_groups=mesh['seq'=8,'head'=4] {'head'}, use_global_device_ids=true, to_apply=%region_5.6 | all-reduce | flops 2048 | bytes 16384 | tf_op jit(solution)/shard_map/psum | solution.py:48
  290.5 26.7 %convolution_bitcast_fusion = f32[4096,2048]{0,1:T(8,128)} fusion(bf16[1024,4096]{1,0:T(8,128)(2,1)} %all-gather.3.cloned.1.call-done, bf16[1024,2048]{1,0:T(8,128)(2,1)} %param.16, f32[2048]{0:T(1024)S(1)} %copy-done.11, f32[1024]{0:T(1024)S(1)} %get-tuple-element.217, bf16[1024,2048]{1,0:T(8,128)(2,1)} %param.17), kind=kOutput, calls=%fused_computation.9 | convolution fusion | flops 17200840704 | bytes 50343936 | tf_op jit(solution)/shard_map/dot_general | solution.py:61
  317.2 0.9 copy-done.6
  318.3 2.3 reduce-window.6
  323.2 0.7 copy.47
  324.6 1.3 subtract_exponential_fusion.1
  325.9 5.5 convolution_convert_fusion.1
  331.4 5.3 convolution_convert_fusion
  336.7 1.0 slice-done.1
  337.7 9.0 %fusion.10 = (bf16[1024,2048]{1,0:T(8,128)(2,1)}, bf16[1024,2048]{1,0:T(8,128)(2,1)}) fusion(bf16[1024,2048]{1,0:T(8,128)(2,1)S(1)} %copy-done.3, bf16[1024,2048]{1,0:T(8,128)(2,1)S(1)} %copy-done.4, f32[1024]{0:T(1024)S(1)} %copy-done.14, f32[1024,2048]{1,0:T(8,128)S(1)} %bitcast.75, f32[1024]{0:T(1024)S(1)} %get-tuple-element.218, f32[2048]{0:T(1024)S(1)} %copy-done.12, ...), kind=kLoop, calls=%fused_computation.22 | loop fusion | flops 46137344 | bytes 25186304 | tf_op jit(solution)/shard_map/convert_element_type | solution.py:57
  346.7 7.0 %copy.45 = bf16[1024,2048]{0,1:T(8,128)(2,1)} copy(bf16[1024,2048]{1,0:T(8,128)(2,1)} %get-tuple-element.214) | data formatting | bytes 8388608 | tf_op jit(solution)/shard_map/convert_element_type | solution.py:58
  353.7 16.3 %fusion.39 = f32[4,32,64,128]{3,2,0,1:T(8,128)} fusion(bf16[32,4,256,128]{3,0,2,1:T(8,128)(2,1)} %bitcast.76, f32[32,4,256]{2,1,0:T(4,128)S(1)} %copy-done.8, bf16[32,8,4,8,256]{4,3,2,1,0:T(8,128)(2,1)} %bitcast.78), kind=kOutput, calls=%fused_computation.52 | convolution fusion | flops 543162368 | bytes 16908288 | tf_op jit(solution)/shard_map/hksp,hksn->hkpn/dot_general | solution.py:104
  370.0 2.5 broadcast_in_dim.23
  372.5 10.1 %while.28 = (s32[]{:T(128)}, f32[32,64,128]{2,1,0:T(8,128)S(1)}, f32[4,32,64,128]{3,2,1,0:T(8,128)}, f32[4,32,64,128]{3,2,0,1:T(8,128)}, f32[4,32]{1,0:T(4,128)S(1)}, /*index=5*/s32[]{:T(128)}, s32[]{:T(128)}, s32[]{:T(128)}) while((s32[]{:T(128)}, f32[32,64,128]{2,1,0:T(8,128)S(1)}, f32[4,32,64,128]{3,2,1,0:T(8,128)}, ...), condition=%wide.region_7.8_spmd.clone, body=%wide.region_6.7_spmd.clone.sunk | while | flops 1048580 | bytes 5243392 | solution.py:111
  372.6 1.1 bitcast_dynamic-update-slice_fusion.2
  373.6 1.4 bitcast_add_fusion.3
  375.1 1.1 bitcast_dynamic-update-slice_fusion.2
  376.2 1.4 bitcast_add_fusion.3
  377.6 1.1 bitcast_dynamic-update-slice_fusion.2
  378.7 1.4 bitcast_add_fusion.3
  380.2 1.1 bitcast_dynamic-update-slice_fusion.2
  381.3 1.4 bitcast_add_fusion.3
  382.7 138.0 %while.29 = (s32[]{:T(128)}, f32[32,64,128]{2,1,0:T(8,128)S(1)}, f32[32]{0:T(128)S(1)}, f32[32,64,128]{2,1,0:T(8,128)S(1)}, s32[]{:T(128)}, /*index=5*/s32[]{:T(128)}) while((s32[]{:T(128)}, f32[32,64,128]{2,1,0:T(8,128)S(1)}, f32[32]{0:T(128)S(1)}, f32[32,64,128]{2,1,0:T(8,128)S(1)}, s32[]{:T(128)}, /*index=5*/s32[]{:T(128)}) %tuple.85), condition=%wide.region_11.12_spmd.clone, body=%wide.region_10.11_spmd.clone.sunk | while | flops 1310723 | bytes 6291703 | solution.py:124
  382.9 1.3 collective-permute-start
  384.2 2.5 collective-permute-done
  387.1 1.3 collective-permute-start
  388.4 19.1 %collective-permute-done = bf16[32,64,128]{2,1,0:T(8,128)(2,1)S(1)} collective-permute-done((bf16[32,64,128]{2,1,0:T(8,128)(2,1)S(1)}, bf16[32,64,128]{2,1,0:T(8,128)(2,1)S(1)}, u32[]{:S(2)}, u32[]{:S(2)}) %collective-permute-start) | collective-permute-done | bytes 524320 | tf_op jit(solution)/shard_map/while/body/eval_jaxpr/ppermute | solution.py:16
  407.8 1.3 collective-permute-start
  409.1 20.8 %collective-permute-done = bf16[32,64,128]{2,1,0:T(8,128)(2,1)S(1)} collective-permute-done((bf16[32,64,128]{2,1,0:T(8,128)(2,1)S(1)}, bf16[32,64,128]{2,1,0:T(8,128)(2,1)S(1)}, u32[]{:S(2)}, u32[]{:S(2)}) %collective-permute-start) | collective-permute-done | bytes 524320 | tf_op jit(solution)/shard_map/while/body/eval_jaxpr/ppermute | solution.py:16
  430.3 1.3 collective-permute-start
  431.6 21.0 %collective-permute-done = bf16[32,64,128]{2,1,0:T(8,128)(2,1)S(1)} collective-permute-done((bf16[32,64,128]{2,1,0:T(8,128)(2,1)S(1)}, bf16[32,64,128]{2,1,0:T(8,128)(2,1)S(1)}, u32[]{:S(2)}, u32[]{:S(2)}) %collective-permute-start) | collective-permute-done | bytes 524320 | tf_op jit(solution)/shard_map/while/body/eval_jaxpr/ppermute | solution.py:16
  452.9 1.3 collective-permute-start
  454.2 21.0 %collective-permute-done = bf16[32,64,128]{2,1,0:T(8,128)(2,1)S(1)} collective-permute-done((bf16[32,64,128]{2,1,0:T(8,128)(2,1)S(1)}, bf16[32,64,128]{2,1,0:T(8,128)(2,1)S(1)}, u32[]{:S(2)}, u32[]{:S(2)}) %collective-permute-start) | collective-permute-done | bytes 524320 | tf_op jit(solution)/shard_map/while/body/eval_jaxpr/ppermute | solution.py:16
  475.5 1.3 collective-permute-start
  476.8 21.0 %collective-permute-done = bf16[32,64,128]{2,1,0:T(8,128)(2,1)S(1)} collective-permute-done((bf16[32,64,128]{2,1,0:T(8,128)(2,1)S(1)}, bf16[32,64,128]{2,1,0:T(8,128)(2,1)S(1)}, u32[]{:S(2)}, u32[]{:S(2)}) %collective-permute-start) | collective-permute-done | bytes 524320 | tf_op jit(solution)/shard_map/while/body/eval_jaxpr/ppermute | solution.py:16
  498.2 1.3 collective-permute-start
  499.5 21.0 %collective-permute-done = bf16[32,64,128]{2,1,0:T(8,128)(2,1)S(1)} collective-permute-done((bf16[32,64,128]{2,1,0:T(8,128)(2,1)S(1)}, bf16[32,64,128]{2,1,0:T(8,128)(2,1)S(1)}, u32[]{:S(2)}, u32[]{:S(2)}) %collective-permute-start) | collective-permute-done | bytes 524320 | tf_op jit(solution)/shard_map/while/body/eval_jaxpr/ppermute | solution.py:16
  520.8 17.2 %fusion.22 = f32[32,4,256,64]{2,3,1,0:T(8,128)} fusion(bf16[32,4,256,128]{3,0,2,1:T(8,128)(2,1)} %bitcast.71, f32[4,32,64,128]{3,2,1,0:T(8,128)} %get-tuple-element.129, f32[32,64,128]{2,1,0:T(8,128)S(1)} %get-tuple-element.131, f32[32,4]{0,1:T(4,128)S(1)} %copy-done.13), kind=kOutput, calls=%fused_computation.38 | convolution fusion | flops 540016640 | bytes 22020608 | tf_op jit(solution)/shard_map/hkpn,hktn->hktp/dot_general | solution.py:127
  538.0 21.0 %fusion.44 = bf16[32,4,8,8,256]{4,3,2,1,0:T(8,128)(2,1)} fusion(bf16[32,8,4,8,256]{4,3,2,1,0:T(8,128)(2,1)} %bitcast.79, f32[32]{0:T(128)S(1)} %copy-done.16, f32[32,4,256,64]{2,3,1,0:T(8,128)} %fusion.22, f32[32,4,256]{2,1,0:T(4,128)S(1)} %copy.53, f32[32,4,256]{2,1,0:T(4,128)S(1)} %copy.43, pred[256,256]{1,0:T(8,128)(4,1)S(1)} %copy-done.9, ...), kind=kOutput, calls=%fused_computation.53 | convolution fusion | flops 3277848576 | bytes 34013312 | tf_op jit(solution)/shard_map/hkts,hksp->hktp/dot_general | solution.py:99
  558.9 4.8 copy.60
  563.8 6.6 copy.55
  570.4 108.2 %reduce-scatter.2.cloned.1.call-done = f32[512,2048]{0,1:T(8,128)} async-done(((f32[4096,2048]{0,1:T(8,128)}), f32[512,2048]{0,1:T(8,128)}) %reduce-scatter.2.cloned.1.call-update) | async-done | bytes 4194320 | tf_op jit(solution)/shard_map/reduce_scatter | solution.py:60
  678.5 4.6 broadcast_multiply_fusion
  683.2 5.3 copy.56
  (78 shorter events, 6.5 us)
Async XLA Ops:
  7.2 318.7 %copy-start = (bf16[1024,8,128]{2,1,0:T(8,128)(2,1)S(1)}, bf16[1024,8,128]{2,1,0:T(8,128)(2,1)}, u32[]{:S(2)}) copy-start(bf16[1024,8,128]{2,1,0:T(8,128)(2,1)} %param.21) | copy-start | bytes 6291460
  7.2 92.9 %all-gather.3.cloned.1.call-start = ((), (), s32[]{:S(2)}) async-start(), calls=%async_computation.1 | async-start | bytes 10485760 | tf_op jit(solution)/shard_map/all_gather | solution.py:34
  7.9 244.9 %all-gather.5.cloned.1.call-start = ((), (), s32[]{:S(2)}) async-start(), calls=%async_computation.2 | async-start | bytes 18874368 | tf_op jit(solution)/shard_map/all_gather | solution.py:45
  8.7 281.8 %copy-start.11 = (f32[2048]{0:T(1024)S(1)}, f32[2048]{0:T(1024)}, u32[]{:S(2)}) copy-start(f32[2048]{0:T(1024)} %param.18) | copy-start | bytes 24580
  8.7 669.9 %reduce-scatter.2.cloned.1.call-start = ((), (), s32[]{:S(2)}) async-start(), calls=%async_computation.3 | async-start | bytes 37748736 | tf_op jit(solution)/shard_map/reduce_scatter | solution.py:60
  317.2 0.9 copy-start.6
  317.2 1.0 copy-start.7
  321.2 0.5 copy-start.15
  323.9 7.4 %copy-start.5 = (bf16[1024,8,128]{2,1,0:T(8,128)(2,1)S(1)}, bf16[1024,8,128]{2,1,0:T(8,128)(2,1)}, u32[]{:S(2)}) copy-start(bf16[1024,8,128]{2,1,0:T(8,128)(2,1)} %param.22) | copy-start | bytes 6291460
  325.9 10.8 %slice-start = ((s8[8388608]{0:T(1024)(128)(4,1)}), s8[4194304]{0:T(1024)(128)(4,1)S(1)}, s32[]{:S(2)}) async-start(s8[8388608]{0:T(1024)(128)(4,1)} %bitcast.74), calls=%async_computation.4 | async-start | bytes 8388608
  325.9 10.8 %copy-start.3 = (bf16[1024,2048]{1,0:T(8,128)(2,1)S(1)}, bf16[1024,2048]{1,0:T(8,128)(2,1)}, u32[]{:S(2)}) copy-start(bf16[1024,2048]{1,0:T(8,128)(2,1)} %param.16) | copy-start | bytes 12582916
  325.9 10.8 %copy-start.4 = (bf16[1024,2048]{1,0:T(8,128)(2,1)S(1)}, bf16[1024,2048]{1,0:T(8,128)(2,1)}, u32[]{:S(2)}) copy-start(bf16[1024,2048]{1,0:T(8,128)(2,1)} %param.17) | copy-start | bytes 12582916
  325.9 10.8 %copy-start.12 = (f32[2048]{0:T(1024)S(1)}, f32[2048]{0:T(1024)}, u32[]{:S(2)}) copy-start(f32[2048]{0:T(1024)} %param.18) | copy-start | bytes 24580
  325.9 10.8 %copy-start.14 = (f32[1024]{0:T(1024)S(1)}, f32[1024]{0:T(1024)}, u32[]{:S(2)}) copy-start(f32[1024]{0:T(1024)} %get-tuple-element.211) | copy-start | bytes 12292
  331.4 6.3 slice-start.1
  346.7 7.0 %copy-start.8 = (f32[32,4,256]{2,1,0:T(4,128)S(1)}, f32[32,4,256]{2,1,0:T(4,128)}, u32[]{:S(2)}) copy-start(f32[32,4,256]{2,1,0:T(4,128)} %copy.47) | copy-start | bytes 393220
  372.5 10.2 %copy-start.2 = (f32[32,64,128]{2,1,0:T(8,128)S(1)}, f32[32,64,128]{2,1,0:T(8,128)}, u32[]{:S(2)}) copy-start(f32[32,64,128]{2,1,0:T(8,128)} %custom-call.1) | copy-start | bytes 3145732
  372.5 10.2 %copy-start.10 = (f32[32]{0:T(128)S(1)}, f32[32]{0:T(128)}, u32[]{:S(2)}) copy-start(f32[32]{0:T(128)} %exp.50) | copy-start | bytes 388
  382.7 138.0 %copy-start.13 = (f32[32,4]{0,1:T(4,128)S(1)}, f32[32,4]{0,1:T(4,128)}, u32[]{:S(2)}) copy-start(f32[32,4]{0,1:T(4,128)} %subtract_exponential_fusion.1) | copy-start | bytes 1540
  382.9 3.8 collective-permute-start
  387.1 20.4 %collective-permute-start = (bf16[32,64,128]{2,1,0:T(8,128)(2,1)S(1)}, bf16[32,64,128]{2,1,0:T(8,128)(2,1)S(1)}, u32[]{:S(2)}, u32[]{:S(2)}) collective-permute-start(bf16[32,64,128]{2,1,0:T(8,128)(2,1)S(1)} %fusion.76), channel_id=1, source_target_pairs={{4,0},{8,4},{12,8},{16,12},{20,16},{24,20},{28,24},{5,1},{9,5},{13... | collective-permute-start | bytes 1572872 | tf_op jit(solution)/shard_map/while/body/eval_jaxpr/ppermute | solution.py:16
  407.8 22.1 %collective-permute-start = (bf16[32,64,128]{2,1,0:T(8,128)(2,1)S(1)}, bf16[32,64,128]{2,1,0:T(8,128)(2,1)S(1)}, u32[]{:S(2)}, u32[]{:S(2)}) collective-permute-start(bf16[32,64,128]{2,1,0:T(8,128)(2,1)S(1)} %fusion.76), channel_id=1, source_target_pairs={{4,0},{8,4},{12,8},{16,12},{20,16},{24,20},{28,24},{5,1},{9,5},{13... | collective-permute-start | bytes 1572872 | tf_op jit(solution)/shard_map/while/body/eval_jaxpr/ppermute | solution.py:16
  430.3 22.3 %collective-permute-start = (bf16[32,64,128]{2,1,0:T(8,128)(2,1)S(1)}, bf16[32,64,128]{2,1,0:T(8,128)(2,1)S(1)}, u32[]{:S(2)}, u32[]{:S(2)}) collective-permute-start(bf16[32,64,128]{2,1,0:T(8,128)(2,1)S(1)} %fusion.76), channel_id=1, source_target_pairs={{4,0},{8,4},{12,8},{16,12},{20,16},{24,20},{28,24},{5,1},{9,5},{13... | collective-permute-start | bytes 1572872 | tf_op jit(solution)/shard_map/while/body/eval_jaxpr/ppermute | solution.py:16
  452.9 22.3 %collective-permute-start = (bf16[32,64,128]{2,1,0:T(8,128)(2,1)S(1)}, bf16[32,64,128]{2,1,0:T(8,128)(2,1)S(1)}, u32[]{:S(2)}, u32[]{:S(2)}) collective-permute-start(bf16[32,64,128]{2,1,0:T(8,128)(2,1)S(1)} %fusion.76), channel_id=1, source_target_pairs={{4,0},{8,4},{12,8},{16,12},{20,16},{24,20},{28,24},{5,1},{9,5},{13... | collective-permute-start | bytes 1572872 | tf_op jit(solution)/shard_map/while/body/eval_jaxpr/ppermute | solution.py:16
  475.5 22.3 %collective-permute-start = (bf16[32,64,128]{2,1,0:T(8,128)(2,1)S(1)}, bf16[32,64,128]{2,1,0:T(8,128)(2,1)S(1)}, u32[]{:S(2)}, u32[]{:S(2)}) collective-permute-start(bf16[32,64,128]{2,1,0:T(8,128)(2,1)S(1)} %fusion.76), channel_id=1, source_target_pairs={{4,0},{8,4},{12,8},{16,12},{20,16},{24,20},{28,24},{5,1},{9,5},{13... | collective-permute-start | bytes 1572872 | tf_op jit(solution)/shard_map/while/body/eval_jaxpr/ppermute | solution.py:16
  498.2 22.3 %collective-permute-start = (bf16[32,64,128]{2,1,0:T(8,128)(2,1)S(1)}, bf16[32,64,128]{2,1,0:T(8,128)(2,1)S(1)}, u32[]{:S(2)}, u32[]{:S(2)}) collective-permute-start(bf16[32,64,128]{2,1,0:T(8,128)(2,1)S(1)} %fusion.76), channel_id=1, source_target_pairs={{4,0},{8,4},{12,8},{16,12},{20,16},{24,20},{28,24},{5,1},{9,5},{13... | collective-permute-start | bytes 1572872 | tf_op jit(solution)/shard_map/while/body/eval_jaxpr/ppermute | solution.py:16
  520.7 17.2 %copy-start.9 = (pred[256,256]{1,0:T(8,128)(4,1)S(1)}, pred[256,256]{1,0:T(8,128)(4,1)}, u32[]{:S(2)}) copy-start(pred[256,256]{1,0:T(8,128)(4,1)} %iota_compare_fusion) | copy-start | bytes 196612
  520.7 17.2 %copy-start.16 = (f32[32]{0:T(128)S(1)}, f32[32]{0:T(128)}, u32[]{:S(2)}) copy-start(f32[32]{0:T(128)} %param.23) | copy-start | bytes 388
  563.8 124.8 %copy-start.1 = (bf16[1024,8,128]{2,1,0:T(8,128)(2,1)S(1)}, bf16[1024,8,128]{2,1,0:T(8,128)(2,1)}, u32[]{:S(2)}) copy-start(bf16[1024,8,128]{2,1,0:T(8,128)(2,1)} %param.21) | copy-start | bytes 6291460
Sparse Core Ops, SparseCore 0:
  9.8 90.1 all-gather.2
  101.7 151.0 all-gather.4
  317.3 361.1 reduce-scatter.1
where the time goes:
time: 700 us; the launch traced here: 695 us
  waiting for transfers between devices  480 us (69%)
  matrix products  119 us (17%)
  other arithmetic  31.1 us (4%)
  local copies, waits for them, and re-layouts  30.7 us (4%)
  between operations  14.2 us (2%)
  blocking collectives  10.5 us (2%)
  starting transfers between devices  9.16 us (1%)
    all_gather x1, waiting for transfers between devices, on_device(): lax.all_gather(out_weight, 'seq', axis=0, tiled=True)  153 us
    ppermute x7, waiting for transfers between devices, shifted(): return lax.ppermute(x, axis, pairs)  126 us
    reduce_scatter x1, waiting for transfers between devices, on_device(): lax.psum_scatter(lax.dot_general(columns, normed, (((0,), (0,)), ((), ())...  108 us
    all_gather x1, waiting for transfers between devices, on_device(): full_grad = lax.all_gather(grad_output, 'head', axis=1, tiled=True)  91.3 us
    dot_general x1, matrix products, on_device(): jnp.dot(columns, lax.all_gather(out_weight, 'seq', axis=0, tiled=True), p...  27.2 us
    dot_general x1, matrix products, on_device(): lax.dot_general(columns, normed, (((0,), (0,)), ((), ())), preferred_elem...  26.7 us
    dot_general x1, matrix products, on_device(): jnp.einsum('hkts,hksp->hktp', block_weights, grad_heads, preferred_elemen...  21 us
    dot_general x1, matrix products, on_device(): jnp.einsum('hkpn,hktn->hktp', carry_low, b_heads, preferred_element_type=...  17.2 us
  transfers between devices with their start and end apart: 10, of which 10 were waited for; matrix products, arithmetic and copies ran while one was open for 16% of the time, Pallas kernels for 0%

commit v1 on v0

--- a/solution.py
+++ b/solution.py
@@ -31,7 +31,12 @@
     tok_rows = ssd_out.shape[0]
     local_width = ssd_out.shape[1]
     total_width = local_width * lax.axis_size("head")
-    full_grad = lax.all_gather(grad_output, "head", axis=1, tiled=True)
+    ring = [grad_output]
+    for hop in range(3):
+        ring.append(lax.ppermute(ring[-1], "head", [(dev, (dev + 1) % 4) for dev in range(4)]))
+    full_grad = jnp.roll(
+        jnp.concatenate(ring[::-1], axis=1), (lax.axis_index("head") + 1) * ring[0].shape[1], axis=1
+    )
     values = ssd_out.astype(jnp.float32)
     gate_values = gate.astype(jnp.float32)
     sigmoid_gate = jax.nn.sigmoid(gate_values)

time: 700 us -> 623 us (0.89)
  waiting for transfers between devices: 480 us -> 382 us
  local copies, waits for them, and re-layouts: 30.7 us -> 44.5 us
    all_gather x1, waiting for transfers between devices: 153 us -> 0.01 us  [on_device(): lax.all_gather(out_weight, 'seq', axis=0, tiled=True)]
    ppermute x0 -> x3, waiting for transfers between devices: none -> 141 us  [on_device(): lax.ppermute(ring[-1], 'head', [(dev, (dev + 1) % 4) for dev in range(4)])]
    all_gather x1 -> x0, waiting for transfers between devices: 91.3 us -> none  [on_device(): full_grad = lax.all_gather(grad_output, 'head', axis=1, tiled=True)]
    unnamed x40 -> x46, local copies, waits for them, and re-layouts: 14.4 us -> 26.5 us
  transfers between devices with their start and end apart: 10 -> 12, of which waited for: 10 -> 11; matrix products, arithmetic and copies ran while one was open for 16% -> 21% of each run, Pallas kernels for 0% -> 0%
where the time goes in v1:
time: 623 us; the launch traced here: 618 us
  waiting for transfers between devices  382 us (61%)
  matrix products  124 us (20%)
  local copies, waits for them, and re-layouts  44.5 us (7%)
  other arithmetic  30.8 us (5%)
  between operations  14.5 us (2%)
  starting transfers between devices  12.9 us (2%)
  blocking collectives  8.16 us (1%)
    ppermute x3, waiting for transfers between devices, on_device(): lax.ppermute(ring[-1], 'head', [(dev, (dev + 1) % 4) for dev in range(4)])  141 us
    ppermute x7, waiting for transfers between devices, shifted(): return lax.ppermute(x, axis, pairs)  130 us
    reduce_scatter x1, waiting for transfers between devices, on_device(): lax.psum_scatter(lax.dot_general(columns, normed, (((0,), (0,)), ((), ())...  111 us
    dot_general x1, matrix products, on_device(): lax.dot_general(columns, normed, (((0,), (0,)), ((), ())), preferred_elem...  31.3 us
    dot_general x1, matrix products, on_device(): jnp.dot(columns, lax.all_gather(out_weight, 'seq', axis=0, tiled=True), p...  27.4 us
    unnamed x46, local copies, waits for them, and re-layouts  26.5 us
    dot_general x1, matrix products, on_device(): jnp.einsum('hkts,hksp->hktp', block_weights, grad_heads, preferred_elemen...  21 us
    dot_general x1, matrix products, on_device(): jnp.einsum('hkpn,hktn->hktp', carry_low, b_heads, preferred_element_type=...  17.2 us
  transfers between devices with their start and end apart: 12, of which 11 were waited for; matrix products, arithmetic and copies ran while one was open for 21% of the time, Pallas kernels for 0%

profile of v1, /device:TPU:0, one launch (start us, length us, event | category | flops | bytes accessed | tf_op | source)
XLA Modules:
  0.0 617.9 jit_solution(13002204339327520066)
XLA Ops:
  8.0 3.0 collective-permute-start.1
  11.0 46.8 %collective-permute-done.1 = bf16[1024,1024]{1,0:T(8,128)(2,1)S(1)} collective-permute-done((bf16[1024,1024]{1,0:T(8,128)(2,1)}, bf16[1024,1024]{1,0:T(8,128)(2,1)S(1)}, u32[]{:S(2)}, u32[]{:S(2)}) %collective-permute-start.1) | collective-permute-done | bytes 2097184 | tf_op jit(solution)/shard_map/ppermute | solution.py:36
  57.8 1.3 copy-done.4
  59.9 47.1 %collective-permute-done.2 = bf16[1024,1024]{1,0:T(8,128)(2,1)} collective-permute-done((bf16[1024,1024]{1,0:T(8,128)(2,1)S(1)}, bf16[1024,1024]{1,0:T(8,128)(2,1)}, u32[]{:S(2)}, u32[]{:S(2)}) %collective-permute-start.2) | collective-permute-done | bytes 2097184 | tf_op jit(solution)/shard_map/ppermute | solution.py:36
  107.0 47.2 %collective-permute-done.3 = bf16[1024,1024]{1,0:T(8,128)(2,1)} collective-permute-done((bf16[1024,1024]{1,0:T(8,128)(2,1)}, bf16[1024,1024]{1,0:T(8,128)(2,1)}, u32[]{:S(2)}, u32[]{:S(2)}) %collective-permute-start.3) | collective-permute-done | bytes 2097184 | tf_op jit(solution)/shard_map/ppermute | solution.py:36
  154.3 3.1 constant_dynamic-update-slice_fusion.7
  157.4 3.1 constant_dynamic-update-slice_fusion.6
  160.5 1.5 constant_dynamic-update-slice_fusion.5
  162.0 1.5 constant_dynamic-update-slice_fusion.4
  163.5 3.1 constant_dynamic-update-slice_fusion.3
  166.6 3.1 constant_dynamic-update-slice_fusion.2
  169.6 1.5 constant_dynamic-update-slice_fusion.1
  171.2 1.5 constant_dynamic-update-slice_fusion
  172.7 27.4 %multiply_reduce_fusion.1 = (f32[1024]{0:T(1024)S(1)}, f32[1024]{0:T(1024)S(1)}, f32[1024,2048]{1,0:T(8,128)}) fusion(bf16[1024,2048]{1,0:T(8,128)(2,1)} %param.16, bf16[1024,2048]{1,0:T(8,128)(2,1)} %param.17, f32[2048]{0:T(1024)S(1)} %copy-done.13, bf16[4096,2048]{1,0:T(8,128)(2,1)} %all-gather.2.cloned.1.call-done, ...), kind=kOutput, calls=%fused_computation.33 | convolution fusion | flops 17205035008 | bytes 41959428 | tf_op jit(solution)/shard_map/dot_general | solution.py:48
  200.1 8.2 %all-reduce = (f32[1024]{0:T(1024)}, f32[1024]{0:T(1024)S(1)}) all-reduce(f32[1024]{0:T(1024)S(1)} %get-tuple-element.187, f32[1024]{0:T(1024)S(1)} %get-tuple-element.186), channel_id=1, replica_groups=mesh['seq'=8,'head'=4] {'head'}, use_global_device_ids=true, to_apply=%region_5.6 | all-reduce | flops 2048 | bytes 16384 | tf_op jit(solution)/shard_map/psum | solution.py:53
  208.3 31.3 %fusion.26 = f32[4096,2048]{1,0:T(8,128)} fusion(bf16[1024,8192]{1,0:T(8,128)(2,1)} %constant_dynamic-update-slice_fusion, s32[]{:T(128)S(6)} %select_n.29, bf16[1024,2048]{1,0:T(8,128)(2,1)} %param.16, f32[2048]{0:T(1024)S(1)} %copy-done.13, f32[1024]{0:T(1024)S(1)} %get-tuple-element.214, bf16[1024,2048]{1,0:T(8,128)(2,1)} %param.17), kind=kOutput, calls=%fused_computation.40 | convolution fusion | flops 17200840704 | bytes 50343940 | tf_op jit(solution)/shard_map/dot_general | solution.py:66
  240.6 2.3 reduce-window.6
  248.0 5.4 convolution_convert_fusion.1
  253.4 5.2 convolution_convert_fusion
  259.4 9.2 %fusion.10 = (bf16[1024,2048]{1,0:T(8,128)(2,1)}, bf16[1024,2048]{1,0:T(8,128)(2,1)}) fusion(bf16[1024,2048]{1,0:T(8,128)(2,1)S(1)} %copy-done.6, bf16[1024,2048]{1,0:T(8,128)(2,1)S(1)} %copy-done.7, f32[1024]{0:T(1024)S(1)} %copy-done.15, f32[1024,2048]{1,0:T(8,128)S(1)} %bitcast.71, f32[1024]{0:T(1024)S(1)} %get-tuple-element.215, f32[2048]{0:T(1024)S(1)} %copy-done.14, ...), kind=kLoop, calls=%fused_computation.21 | loop fusion | flops 46137344 | bytes 25186304 | tf_op jit(solution)/shard_map/convert_element_type | solution.py:62
  268.6 6.5 %copy.43 = bf16[1024,2048]{0,1:T(8,128)(2,1)} copy(bf16[1024,2048]{1,0:T(8,128)(2,1)} %get-tuple-element.211) | data formatting | bytes 8388608 | tf_op jit(solution)/shard_map/convert_element_type | solution.py:63
  275.0 16.3 %fusion.43 = f32[4,32,64,128]{3,2,0,1:T(8,128)} fusion(bf16[32,4,256,128]{3,0,2,1:T(8,128)(2,1)} %bitcast.72, f32[32,4,256]{2,1,0:T(4,128)S(1)} %copy-done.12, bf16[32,8,4,8,256]{4,3,2,1,0:T(8,128)(2,1)} %bitcast.74), kind=kOutput, calls=%fused_computation.55 | convolution fusion | flops 543162368 | bytes 16908288 | tf_op jit(solution)/shard_map/hksp,hksn->hkpn/dot_general | solution.py:109
  291.4 2.5 broadcast_in_dim.23
  293.9 10.0 %while.28 = (s32[]{:T(128)}, f32[32,64,128]{2,1,0:T(8,128)S(1)}, f32[4,32,64,128]{3,2,1,0:T(8,128)}, f32[4,32,64,128]{3,2,0,1:T(8,128)}, f32[4,32]{1,0:T(4,128)S(1)}, /*index=5*/s32[]{:T(128)}, s32[]{:T(128)}, s32[]{:T(128)}) while((s32[]{:T(128)}, f32[32,64,128]{2,1,0:T(8,128)S(1)}, f32[4,32,64,128]{3,2,1,0:T(8,128)}, ...), condition=%wide.region_7.8_spmd.clone, body=%wide.region_6.7_spmd.clone.sunk | while | flops 1048580 | bytes 5243392 | solution.py:116
  295.0 1.4 bitcast_add_fusion.3
  297.5 1.4 bitcast_add_fusion.3
  300.0 1.4 bitcast_add_fusion.3
  302.5 1.4 bitcast_add_fusion.3
  303.9 141.2 %while.29 = (s32[]{:T(128)}, f32[32,64,128]{2,1,0:T(8,128)S(1)}, f32[32]{0:T(128)S(1)}, f32[32,64,128]{2,1,0:T(8,128)S(1)}, s32[]{:T(128)}, /*index=5*/s32[]{:T(128)}) while((s32[]{:T(128)}, f32[32,64,128]{2,1,0:T(8,128)S(1)}, f32[32]{0:T(128)S(1)}, f32[32,64,128]{2,1,0:T(8,128)S(1)}, s32[]{:T(128)}, /*index=5*/s32[]{:T(128)}) %tuple.80), condition=%wide.region_11.12_spmd.clone, body=%wide.region_10.11_spmd.clone.sunk | while | flops 1310723 | bytes 6291703 | solution.py:129
  304.1 1.3 collective-permute-start
  305.4 2.5 collective-permute-done
  308.3 1.3 collective-permute-start
  309.6 21.3 %collective-permute-done = bf16[32,64,128]{2,1,0:T(8,128)(2,1)S(1)} collective-permute-done((bf16[32,64,128]{2,1,0:T(8,128)(2,1)S(1)}, bf16[32,64,128]{2,1,0:T(8,128)(2,1)S(1)}, u32[]{:S(2)}, u32[]{:S(2)}) %collective-permute-start) | collective-permute-done | bytes 524320 | tf_op jit(solution)/shard_map/while/body/eval_jaxpr/ppermute | solution.py:16
  331.2 1.3 collective-permute-start
  332.5 21.5 %collective-permute-done = bf16[32,64,128]{2,1,0:T(8,128)(2,1)S(1)} collective-permute-done((bf16[32,64,128]{2,1,0:T(8,128)(2,1)S(1)}, bf16[32,64,128]{2,1,0:T(8,128)(2,1)S(1)}, u32[]{:S(2)}, u32[]{:S(2)}) %collective-permute-start) | collective-permute-done | bytes 524320 | tf_op jit(solution)/shard_map/while/body/eval_jaxpr/ppermute | solution.py:16
  354.3 1.3 collective-permute-start
  355.6 21.2 %collective-permute-done = bf16[32,64,128]{2,1,0:T(8,128)(2,1)S(1)} collective-permute-done((bf16[32,64,128]{2,1,0:T(8,128)(2,1)S(1)}, bf16[32,64,128]{2,1,0:T(8,128)(2,1)S(1)}, u32[]{:S(2)}, u32[]{:S(2)}) %collective-permute-start) | collective-permute-done | bytes 524320 | tf_op jit(solution)/shard_map/while/body/eval_jaxpr/ppermute | solution.py:16
  377.1 1.3 collective-permute-start
  378.4 20.9 %collective-permute-done = bf16[32,64,128]{2,1,0:T(8,128)(2,1)S(1)} collective-permute-done((bf16[32,64,128]{2,1,0:T(8,128)(2,1)S(1)}, bf16[32,64,128]{2,1,0:T(8,128)(2,1)S(1)}, u32[]{:S(2)}, u32[]{:S(2)}) %collective-permute-start) | collective-permute-done | bytes 524320 | tf_op jit(solution)/shard_map/while/body/eval_jaxpr/ppermute | solution.py:16
  399.7 1.3 collective-permute-start
  401.0 21.1 %collective-permute-done = bf16[32,64,128]{2,1,0:T(8,128)(2,1)S(1)} collective-permute-done((bf16[32,64,128]{2,1,0:T(8,128)(2,1)S(1)}, bf16[32,64,128]{2,1,0:T(8,128)(2,1)S(1)}, u32[]{:S(2)}, u32[]{:S(2)}) %collective-permute-start) | collective-permute-done | bytes 524320 | tf_op jit(solution)/shard_map/while/body/eval_jaxpr/ppermute | solution.py:16
  423.7 21.1 %collective-permute-done = bf16[32,64,128]{2,1,0:T(8,128)(2,1)S(1)} collective-permute-done((bf16[32,64,128]{2,1,0:T(8,128)(2,1)S(1)}, bf16[32,64,128]{2,1,0:T(8,128)(2,1)S(1)}, u32[]{:S(2)}, u32[]{:S(2)}) %collective-permute-start) | collective-permute-done | bytes 524320 | tf_op jit(solution)/shard_map/while/body/eval_jaxpr/ppermute | solution.py:16
  445.1 17.2 %fusion.22 = f32[32,4,256,64]{2,3,1,0:T(8,128)} fusion(bf16[32,4,256,128]{3,0,2,1:T(8,128)(2,1)} %bitcast.67, f32[4,32,64,128]{3,2,1,0:T(8,128)} %get-tuple-element.129, f32[32,64,128]{2,1,0:T(8,128)S(1)} %get-tuple-element.131, f32[32,4]{0,1:T(4,128)S(1)} %subtract_exponential_fusion.1), kind=kOutput, calls=%fused_computation.37 | convolution fusion | flops 540016640 | bytes 22020608 | tf_op jit(solution)/shard_map/hkpn,hktn->hktp/dot_general | solution.py:132
  462.3 21.0 %fusion.48 = bf16[32,4,8,8,256]{4,3,2,1,0:T(8,128)(2,1)} fusion(bf16[32,8,4,8,256]{4,3,2,1,0:T(8,128)(2,1)} %bitcast.75, f32[32]{0:T(128)S(1)} %copy-done.16, f32[32,4,256,64]{2,3,1,0:T(8,128)} %fusion.22, f32[32,4,256]{2,1,0:T(4,128)S(1)} %copy.51, f32[32,4,256]{2,1,0:T(4,128)S(1)} %copy.41, pred[256,256]{1,0:T(8,128)(4,1)S(1)} %iota_compare_fusion, ...), kind=kOutput, calls=%fused_computation.56 | convolution fusion | flops 3277848576 | bytes 34013312 | tf_op jit(solution)/shard_map/hkts,hksp->hktp/dot_general | solution.py:104
  483.4 4.8 copy.57
  488.2 6.6 %copy.53 = bf16[1024,2048]{1,0:T(8,128)(2,1)} copy(bf16[1024,2048]{0,1:T(8,128)(2,1)} %bitcast.69) | data formatting | bytes 8388608
  494.8 111.0 %reduce-scatter.2.cloned.1.call-done = f32[512,2048]{1,0:T(8,128)} async-done(((f32[4096,2048]{1,0:T(8,128)}), f32[512,2048]{1,0:T(8,128)}) %reduce-scatter.2.cloned.1.call-update) | async-done | bytes 4194320 | tf_op jit(solution)/shard_map/reduce_scatter | solution.py:65
  605.8 5.0 broadcast_multiply_fusion
  (88 shorter events, 15.9 us)
Async XLA Ops:
  7.2 240.8 %copy-start = (bf16[1024,8,128]{2,1,0:T(8,128)(2,1)S(1)}, bf16[1024,8,128]{2,1,0:T(8,128)(2,1)}, u32[]{:S(2)}) copy-start(bf16[1024,8,128]{2,1,0:T(8,128)(2,1)} %param.21) | copy-start | bytes 6291460
  7.2 165.5 %all-gather.2.cloned.1.call-start = ((), (), s32[]{:S(2)}) async-start(), calls=%async_computation.1 | async-start | bytes 18874368 | tf_op jit(solution)/shard_map/all_gather | solution.py:50
  7.9 597.9 %reduce-scatter.2.cloned.1.call-start = ((), (), s32[]{:S(2)}) async-start(), calls=%async_computation.2 | async-start | bytes 37748736 | tf_op jit(solution)/shard_map/reduce_scatter | solution.py:65
  8.0 49.8 %collective-permute-start.1 = (bf16[1024,1024]{1,0:T(8,128)(2,1)}, bf16[1024,1024]{1,0:T(8,128)(2,1)S(1)}, u32[]{:S(2)}, u32[]{:S(2)}) collective-permute-start(bf16[1024,1024]{1,0:T(8,128)(2,1)} %param.14), channel_id=1, source_target_pairs={{0,1},{1,2},{2,3},{3,0},{4,5},{5,6},{6,7},{7,4},{8,9},{9,10},{10,1... | collective-permute-start | bytes 6291464 | tf_op jit(solution)/shard_map/ppermute | solution.py:36
  57.8 1.3 copy-start.4
  59.1 47.9 %collective-permute-start.2 = (bf16[1024,1024]{1,0:T(8,128)(2,1)S(1)}, bf16[1024,1024]{1,0:T(8,128)(2,1)}, u32[]{:S(2)}, u32[]{:S(2)}) collective-permute-start(bf16[1024,1024]{1,0:T(8,128)(2,1)S(1)} %collective-permute-done.1), channel_id=1, source_target_pairs={{0,1},{1,2},{2,3},{3,0},{4,5},{5,6},{6,7},{7,4},{8,9},{9,10},{10,1... | collective-permute-start | bytes 6291464 | tf_op jit(solution)/shard_map/ppermute | solution.py:36
  107.0 47.3 %collective-permute-start.3 = (bf16[1024,1024]{1,0:T(8,128)(2,1)}, bf16[1024,1024]{1,0:T(8,128)(2,1)}, u32[]{:S(2)}, u32[]{:S(2)}) collective-permute-start(bf16[1024,1024]{1,0:T(8,128)(2,1)} %collective-permute-done.2), channel_id=1, source_target_pairs={{0,1},{1,2},{2,3},{3,0},{4,5},{5,6},{6,7},{7,4},{8,9},{9,10},{10,1... | collective-permute-start | bytes 6291464 | tf_op jit(solution)/shard_map/ppermute | solution.py:36
  107.0 53.5 %copy-start.5 = (bf16[1024,1024]{1,0:T(8,128)(2,1)S(1)}, bf16[1024,1024]{1,0:T(8,128)(2,1)}, u32[]{:S(2)}) copy-start(bf16[1024,1024]{1,0:T(8,128)(2,1)} %copy-done.4) | copy-start | bytes 6291460
  107.0 55.0 %copy-start.3 = (bf16[1024,1024]{1,0:T(8,128)(2,1)S(1)}, bf16[1024,1024]{1,0:T(8,128)(2,1)}, u32[]{:S(2)}) copy-start(bf16[1024,1024]{1,0:T(8,128)(2,1)} %param.14) | copy-start | bytes 6291460
  163.5 9.2 %copy-start.13 = (f32[2048]{0:T(1024)S(1)}, f32[2048]{0:T(1024)}, u32[]{:S(2)}) copy-start(f32[2048]{0:T(1024)} %param.18) | copy-start | bytes 24580
  239.6 0.9 copy-start.9
  239.6 6.8 %copy-start.10 = (f32[32,1024]{1,0:T(8,128)S(1)}, f32[32,1024]{1,0:T(8,128)}, u32[]{:S(2)}) copy-start(f32[32,1024]{1,0:T(8,128)} %param.19) | copy-start | bytes 393220
  247.1 6.4 %copy-start.8 = (bf16[1024,8,128]{2,1,0:T(8,128)(2,1)S(1)}, bf16[1024,8,128]{2,1,0:T(8,128)(2,1)}, u32[]{:S(2)}) copy-start(bf16[1024,8,128]{2,1,0:T(8,128)(2,1)} %param.22) | copy-start | bytes 6291460
  247.9 10.7 %slice-start = ((s8[8388608]{0:T(1024)(128)(4,1)}), s8[4194304]{0:T(1024)(128)(4,1)S(1)}, s32[]{:S(2)}) async-start(s8[8388608]{0:T(1024)(128)(4,1)} %bitcast.70), calls=%async_computation.3 | async-start | bytes 8388608
  247.9 10.7 %copy-start.6 = (bf16[1024,2048]{1,0:T(8,128)(2,1)S(1)}, bf16[1024,2048]{1,0:T(8,128)(2,1)}, u32[]{:S(2)}) copy-start(bf16[1024,2048]{1,0:T(8,128)(2,1)} %param.16) | copy-start | bytes 12582916
  248.0 10.7 %copy-start.7 = (bf16[1024,2048]{1,0:T(8,128)(2,1)S(1)}, bf16[1024,2048]{1,0:T(8,128)(2,1)}, u32[]{:S(2)}) copy-start(bf16[1024,2048]{1,0:T(8,128)(2,1)} %param.17) | copy-start | bytes 12582916
  248.0 10.7 %copy-start.14 = (f32[2048]{0:T(1024)S(1)}, f32[2048]{0:T(1024)}, u32[]{:S(2)}) copy-start(f32[2048]{0:T(1024)} %param.18) | copy-start | bytes 24580
  248.0 10.7 %copy-start.15 = (f32[1024]{0:T(1024)S(1)}, f32[1024]{0:T(1024)}, u32[]{:S(2)}) copy-start(f32[1024]{0:T(1024)} %get-tuple-element.208) | copy-start | bytes 12292
  253.4 6.0 slice-start.1
  268.6 6.5 %copy-start.12 = (f32[32,4,256]{2,1,0:T(4,128)S(1)}, f32[32,4,256]{2,1,0:T(4,128)}, u32[]{:S(2)}) copy-start(f32[32,4,256]{2,1,0:T(4,128)} %copy.45) | copy-start | bytes 393220
  293.9 10.0 %copy-start.2 = (f32[32,64,128]{2,1,0:T(8,128)S(1)}, f32[32,64,128]{2,1,0:T(8,128)}, u32[]{:S(2)}) copy-start(f32[32,64,128]{2,1,0:T(8,128)} %custom-call.1) | copy-start | bytes 3145732
  304.1 3.8 collective-permute-start
  308.3 22.6 %collective-permute-start = (bf16[32,64,128]{2,1,0:T(8,128)(2,1)S(1)}, bf16[32,64,128]{2,1,0:T(8,128)(2,1)S(1)}, u32[]{:S(2)}, u32[]{:S(2)}) collective-permute-start(bf16[32,64,128]{2,1,0:T(8,128)(2,1)S(1)} %fusion.80), channel_id=1, source_target_pairs={{4,0},{8,4},{12,8},{16,12},{20,16},{24,20},{28,24},{5,1},{9,5},{13... | collective-permute-start | bytes 1572872 | tf_op jit(solution)/shard_map/while/body/eval_jaxpr/ppermute | solution.py:16
  331.2 22.8 %collective-permute-start = (bf16[32,64,128]{2,1,0:T(8,128)(2,1)S(1)}, bf16[32,64,128]{2,1,0:T(8,128)(2,1)S(1)}, u32[]{:S(2)}, u32[]{:S(2)}) collective-permute-start(bf16[32,64,128]{2,1,0:T(8,128)(2,1)S(1)} %fusion.80), channel_id=1, source_target_pairs={{4,0},{8,4},{12,8},{16,12},{20,16},{24,20},{28,24},{5,1},{9,5},{13... | collective-permute-start | bytes 1572872 | tf_op jit(solution)/shard_map/while/body/eval_jaxpr/ppermute | solution.py:16
  354.3 22.5 %collective-permute-start = (bf16[32,64,128]{2,1,0:T(8,128)(2,1)S(1)}, bf16[32,64,128]{2,1,0:T(8,128)(2,1)S(1)}, u32[]{:S(2)}, u32[]{:S(2)}) collective-permute-start(bf16[32,64,128]{2,1,0:T(8,128)(2,1)S(1)} %fusion.80), channel_id=1, source_target_pairs={{4,0},{8,4},{12,8},{16,12},{20,16},{24,20},{28,24},{5,1},{9,5},{13... | collective-permute-start | bytes 1572872 | tf_op jit(solution)/shard_map/while/body/eval_jaxpr/ppermute | solution.py:16
  377.1 22.2 %collective-permute-start = (bf16[32,64,128]{2,1,0:T(8,128)(2,1)S(1)}, bf16[32,64,128]{2,1,0:T(8,128)(2,1)S(1)}, u32[]{:S(2)}, u32[]{:S(2)}) collective-permute-start(bf16[32,64,128]{2,1,0:T(8,128)(2,1)S(1)} %fusion.80), channel_id=1, source_target_pairs={{4,0},{8,4},{12,8},{16,12},{20,16},{24,20},{28,24},{5,1},{9,5},{13... | collective-permute-start | bytes 1572872 | tf_op jit(solution)/shard_map/while/body/eval_jaxpr/ppermute | solution.py:16
  399.7 22.4 %collective-permute-start = (bf16[32,64,128]{2,1,0:T(8,128)(2,1)S(1)}, bf16[32,64,128]{2,1,0:T(8,128)(2,1)S(1)}, u32[]{:S(2)}, u32[]{:S(2)}) collective-permute-start(bf16[32,64,128]{2,1,0:T(8,128)(2,1)S(1)} %fusion.80), channel_id=1, source_target_pairs={{4,0},{8,4},{12,8},{16,12},{20,16},{24,20},{28,24},{5,1},{9,5},{13... | collective-permute-start | bytes 1572872 | tf_op jit(solution)/shard_map/while/body/eval_jaxpr/ppermute | solution.py:16
  422.4 22.4 %collective-permute-start = (bf16[32,64,128]{2,1,0:T(8,128)(2,1)S(1)}, bf16[32,64,128]{2,1,0:T(8,128)(2,1)S(1)}, u32[]{:S(2)}, u32[]{:S(2)}) collective-permute-start(bf16[32,64,128]{2,1,0:T(8,128)(2,1)S(1)} %fusion.80), channel_id=1, source_target_pairs={{4,0},{8,4},{12,8},{16,12},{20,16},{24,20},{28,24},{5,1},{9,5},{13... | collective-permute-start | bytes 1572872 | tf_op jit(solution)/shard_map/while/body/eval_jaxpr/ppermute | solution.py:16
  445.1 17.3 %copy-start.11 = (f32[32,4,256]{2,1,0:T(4,128)S(1)}, f32[32,4,256]{2,1,0:T(4,128)}, u32[]{:S(2)}) copy-start(f32[32,4,256]{2,1,0:T(4,128)} %mul.168) | copy-start | bytes 393220
  445.1 17.3 %copy-start.16 = (f32[32]{0:T(128)S(1)}, f32[32]{0:T(128)}, u32[]{:S(2)}) copy-start(f32[32]{0:T(128)} %param.23) | copy-start | bytes 388
  488.2 122.6 %copy-start.1 = (bf16[1024,8,128]{2,1,0:T(8,128)(2,1)S(1)}, bf16[1024,8,128]{2,1,0:T(8,128)(2,1)}, u32[]{:S(2)}) copy-start(bf16[1024,8,128]{2,1,0:T(8,128)(2,1)} %param.21) | copy-start | bytes 6291460
Sparse Core Ops, SparseCore 0:
  9.6 153.7 all-gather.1
  239.7 366.0 reduce-scatter.1
